TPU v7x, 128 devices: a whole 4x4x4 slice. The times are simulated.
128 devices in a mesh: prow: 8 (over x, y_lo), pcol: 16 (over y_hi, z, core).
Axes of the slice: x: 4, y: 4 (y_hi: 2, y_lo: 2; y = y_hi * 2 + y_lo), z: 4, core: 2. Of those that a mesh axis runs over, the one named last changes fastest.
Arguments:
- inverse_top: bfloat16 [128, 128, 128, 128], P('prow', 'pcol'), may hold values from -6 to 6
- rows_one: int32 [16, 64], replicated, may hold values from 0 to 127, as said below
- panel_one: bfloat16 [16, 64, 128, 128], P('pcol', 'prow'), may hold values from -0.0625 to 0.0625
- base_one: float32 [16, 128, 128], P('pcol'), may hold values from -6 to 6
- parent_two: int32 [16], replicated, may hold values from 0 to 15
- order_two: int32 [16, 64], replicated, may hold values from 0 to 63, as said below
- panel_two: bfloat16 [16, 64, 128, 128], P('pcol', 'prow'), may hold values from -0.0625 to 0.0625
- link_two: bfloat16 [16, 128, 128], P('pcol'), may hold values from -0.5 to 0.5
- base_two: float32 [16, 128, 128], P('pcol'), may hold values from -6 to 6
Outputs:
- column_one: bfloat16 [16, 64, 128, 128], P('pcol', 'prow')
- diagonal_one: bfloat16 [16, 128, 128], P('pcol')
- column_two: bfloat16 [16, 64, 128, 128], P('pcol', 'prow')
- upper_two: bfloat16 [16, 128, 128], P('pcol')
- diagonal_two: bfloat16 [16, 128, 128], P('pcol')
Inputs may be any that keep to these rules, and one draw needn't show every extreme that they name: For every supernode k and process row p, rows_one[k, p * 8] to rows_one[k, p * 8 + 7] are 8 distinct ancestors between p * 16 and p * 16 + 15. In every draw some process column c holds 8 ancestors (ancestor // 8 == c) of every level-one supernode. Each block order_two[k, p * 8] to order_two[k, p * 8 + 7] is a permutation of p * 8 to p * 8 + 7.
All inputs are finite; a program needn't handle non-finite values.
Results may differ from a plain program's by a relative error of at most 0.024.
Values may be sent and summed in bfloat16 or wider, within the bound.
A program may use at most 192 MiB of HBM per device.

v0:
```python
import jax
import jax.numpy as jnp
from jax import lax
from jax.sharding import PartitionSpec as P


def slot_positions(rows_all, dests, width, capacity):
    owner = rows_all // width
    length = rows_all.shape[1]
    positions = jnp.arange(length, dtype=jnp.int32)
    same_owner = owner[:, :, None] == owner[:, None, :]
    earlier = positions[None, None, :] < positions[None, :, None]
    ranking = jnp.sum(jnp.logical_and(same_owner, earlier), axis=2)
    slot_ids = jnp.arange(capacity, dtype=jnp.int32)
    matches = jnp.logical_and(
        owner[None, :, None, :] == dests[:, None, None, None],
        ranking[None, :, None, :] == slot_ids[None, None, :, None],
    )
    where_at = jnp.sum(jnp.where(matches, positions, 0), axis=3)
    present = jnp.any(matches, axis=3)
    return (where_at, present)


def pack_panels(full_panel, my_rows, width, capacity, columns):
    where_at, present = slot_positions(
        my_rows, jnp.arange(columns, dtype=jnp.int32), width, capacity
    )
    children = jnp.arange(my_rows.shape[0], dtype=jnp.int32)[None, :, None]
    selected = full_panel[children, where_at]
    return jnp.where(present[:, :, :, None, None], selected, jnp.zeros((), selected.dtype))


def local_indices(rows_all, prow_at, pcol_at, per_row, height, width):
    where_at, present = slot_positions(rows_all, jnp.reshape(pcol_at, (1,)), width, per_row)
    targets = jnp.take_along_axis(rows_all, where_at[0], axis=1)
    col_local = jnp.where(present[0], targets - pcol_at * width, 0)
    row_local = lax.dynamic_slice_in_dim(rows_all, prow_at * per_row, per_row, 1) - prow_at * height
    return (row_local, col_local)


def tile_products(inverse_local, received, row_local, col_local):
    blocks = inverse_local[row_local[:, :, None], col_local[:, None, :]]
    return jnp.einsum("kabij,kbjl->kail", blocks, received, preferred_element_type=jnp.float32)


def flatten_received(received):
    return received.reshape((received.shape[0] * received.shape[1],) + received.shape[2:])


def local(
    inverse_top, rows_one, panel_one, base_one, parent_two, order_two, panel_two, link_two, base_two
):
    per_col = panel_one.shape[0]
    per_row = panel_one.shape[1]
    height = inverse_top.shape[0]
    width = inverse_top.shape[1]
    columns = lax.axis_size("pcol")
    prow_at = lax.axis_index("prow")
    pcol_at = lax.axis_index("pcol")
    rows_two = jnp.take_along_axis(rows_one[parent_two], order_two, axis=1)
    mine_one = lax.dynamic_slice_in_dim(rows_one, pcol_at * per_col, per_col, 0)
    mine_two = lax.dynamic_slice_in_dim(rows_two, pcol_at * per_col, per_col, 0)
    row_one, col_one = local_indices(rows_one, prow_at, pcol_at, per_row, height, width)
    row_two, col_two = local_indices(rows_two, prow_at, pcol_at, per_row, height, width)
    full_one = lax.all_gather(panel_one, "prow", axis=1, tiled=True)
    outgoing_one = pack_panels(full_one, mine_one, width, per_row, columns)
    received_one = lax.all_to_all(outgoing_one, "pcol", split_axis=0, concat_axis=0, tiled=True)
    flat_one = flatten_received(received_one)
    summed_one = lax.psum_scatter(
        tile_products(inverse_top, flat_one, row_one, col_one).astype(jnp.bfloat16),
        "pcol",
        scatter_dimension=0,
        tiled=True,
    ).astype(jnp.float32)
    full_two = lax.all_gather(panel_two, "prow", axis=1, tiled=True)
    outgoing_two = pack_panels(full_two, mine_two, width, per_row, columns)
    received_two = lax.all_to_all(outgoing_two, "pcol", split_axis=0, concat_axis=0, tiled=True)
    flat_two = flatten_received(received_two)
    summed_two = lax.psum_scatter(
        tile_products(inverse_top, flat_two, row_two, col_two).astype(jnp.bfloat16),
        "pcol",
        scatter_dimension=0,
        tiled=True,
    ).astype(jnp.float32)
    column_one = (-summed_one).astype(jnp.bfloat16)
    diag_part = jnp.einsum(
        "cmij,cmil->cjl", panel_one, column_one, preferred_element_type=jnp.float32
    )
    diagonal_one = (
        base_one - lax.psum(diag_part.astype(jnp.bfloat16), "prow").astype(jnp.float32)
    ).astype(jnp.bfloat16)
    all_cols, all_diag = (
        lax.all_gather(column_one, "pcol", axis=0, tiled=True),
        lax.all_gather(diagonal_one, "pcol", axis=0, tiled=True),
    )
    my_parent = lax.dynamic_slice_in_dim(parent_two, pcol_at * per_col, per_col, 0)
    my_order = (
        lax.dynamic_slice(order_two, (pcol_at * per_col, prow_at * per_row), (per_col, per_row))
        - prow_at * per_row
    )
    near_cols = all_cols[my_parent[:, None], my_order]
    near_diag = all_diag[my_parent]
    carried = jnp.einsum("cmij,cjl->cmil", near_cols, link_two, preferred_element_type=jnp.float32)
    column_two = (-(summed_two + carried)).astype(jnp.bfloat16)
    upper_part = jnp.einsum(
        "cmij,cmil->cjl", near_cols, panel_two, preferred_element_type=jnp.float32
    )
    parent_term = jnp.einsum(
        "cij,cjl->cil", near_diag, link_two, preferred_element_type=jnp.float32
    )
    upper_total = lax.psum(upper_part.astype(jnp.bfloat16), "prow").astype(jnp.float32)
    upper_two = (-(parent_term + upper_total)).astype(jnp.bfloat16)
    lower_part = jnp.einsum(
        "cmij,cmil->cjl", panel_two, column_two, preferred_element_type=jnp.float32
    )
    lower_total = lax.psum(lower_part.astype(jnp.bfloat16), "prow").astype(jnp.float32)
    link_term = jnp.einsum("cij,cil->cjl", link_two, upper_two, preferred_element_type=jnp.float32)
    diagonal_two = (base_two - link_term - lower_total).astype(jnp.bfloat16)
    return (column_one, diagonal_one, column_two, upper_two, diagonal_two)


def solution(mesh):
    return jax.shard_map(
        local,
        mesh=mesh,
        in_specs=(
            P("prow", "pcol", None, None),
            P(),
            P("pcol", "prow", None, None),
            P("pcol", None, None),
            P(),
            P(),
            P("pcol", "prow", None, None),
            P("pcol", None, None),
            P("pcol", None, None),
        ),
        out_specs=(
            P("pcol", "prow", None, None),
            P("pcol", None, None),
            P("pcol", "prow", None, None),
            P("pcol", None, None),
            P("pcol", None, None),
        ),
        check_vma=False,
    )
```

profile of v0, /device:TPU:8, one launch (start us, length us, event | category | flops | bytes accessed | tf_op | source)
XLA Modules:
  0.0 582.9 jit_solution(2834945553307721107)
XLA Ops:
  7.2 0.7 all-gather.4.cloned.1.call-update
  7.9 0.7 fusion.64
  8.6 0.2 convert_reduce_fusion.3
  8.8 0.4 fusion.28
  9.4 0.1 reshape.639
  9.4 0.4 and_reduce_fusion.1
  9.8 52.6 %all-gather.4.cloned.1.call-done = bf16[1,64,128,128]{3,2,0,1:T(8,128)(2,1)} async-done(((bf16[1,8,128,128]{3,2,0,1:T(8,128)(2,1)}), bf16[1,64,128,128]{3,2,0,1:T(8,128)(2,1)}) %all-gather.4.cloned.1.call-update) | async-done | bytes 2097168 | tf_op jit(solution)/shard_map/all_gather | solution.py:65
  62.4 4.6 gather_fusion.1
  67.0 4.6 broadcast_select_fusion.1
  71.6 6.9 %all-to-all-start = ((bf16[16,1,8,128,128]{4,3,2,1,0:T(8,128)(2,1)}), bf16[16,1,8,128,128]{4,3,2,1,0:T(8,128)(2,1)}, u32[]{:S(2)}, u32[]{:S(2)}) async-start(bf16[16,1,8,128,128]{4,3,2,1,0:T(8,128)(2,1)} %broadcast_select_fusion.1), calls=%async_computation | async-start | bytes 8388608 | tf_op jit(solution)/shard_map/all_to_all | solution.py:67
  78.6 0.6 gather_fusion.2
  79.2 7.1 %gather_fusion.6 = s32[1024]{0:T(1024)S(1)} fusion(s32[16,64]{1,0:T(8,128)S(1)} %gather_fusion.2, s32[1024]{0:T(1024)S(1)} %reshape.675), kind=kCustom, calls=%fused_computation.8 | custom fusion | bytes 16384 | tf_op jit(solution)/shard_map/jit(take_along_axis)/gather | solution.py:60
  86.4 0.9 convert_reduce_fusion
  87.3 0.3 select_reduce_fusion.1
  87.9 0.1 reshape.701
  88.0 1.3 gather_fusion.7
  89.2 0.1 reshape.704
  89.3 0.1 fusion.45
  89.4 0.4 fusion.31
  89.9 0.1 reshape.631
  90.0 23.3 %gather_fusion = bf16[1024,128,128]{2,1,0:T(8,128)(2,1)} fusion(bf16[16,8,128,128]{3,2,1,0:T(8,128)(2,1)} %param.11, s32[1024]{0:T(1024)S(1)} %reshape.631), kind=kCustom, calls=%fused_computation.2 | custom fusion | bytes 67117056 | tf_op jit(solution)/shard_map/gather | solution.py:42
  113.3 18.1 %all-to-all-done = bf16[16,1,8,128,128]{4,3,2,1,0:T(8,128)(2,1)} async-done(((bf16[16,1,8,128,128]{4,3,2,1,0:T(8,128)(2,1)}), bf16[16,1,8,128,128]{4,3,2,1,0:T(8,128)(2,1)}, u32[]{:S(2)}, u32[]{:S(2)}) %all-to-all-start) | async-done | bytes 4194336 | tf_op jit(solution)/shard_map/all_to_all | solution.py:67
  131.4 17.7 %bitcast_convert_fusion.1 = bf16[16,8,128,128]{3,2,1,0:T(8,128)(2,1)} fusion(bf16[16,8,8,128,128]{4,3,2,1,0:T(8,128)(2,1)} %bitcast.161, bf16[16,1,8,128,128]{4,3,2,1,0:T(8,128)(2,1)} %all-to-all-done), kind=kOutput, calls=%fused_computation.10 | convolution fusion | flops 4297064448 | bytes 41943040 | tf_op jit(solution)/shard_map/kabij,kbjl->kail/dot_general | solution.py:43
  149.2 0.7 all-gather.6.cloned.1.call-update
  149.9 0.2 convert_reduce_fusion.2
  150.1 89.4 %reduce-scatter.3.cloned.1.call-done = bf16[1,8,128,128]{3,2,1,0:T(8,128)(2,1)} async-done(((bf16[16,8,128,128]{3,2,1,0:T(8,128)(2,1)}), bf16[1,8,128,128]{3,2,1,0:T(8,128)(2,1)}) %reduce-scatter.3.cloned.1.call-update) | async-done | bytes 262160 | tf_op jit(solution)/shard_map/reduce_scatter | solution.py:69
  239.5 1.7 negate_convert_fusion
  241.2 0.4 fusion.29
  241.7 0.1 reshape.661
  241.8 0.4 and_reduce_fusion
  242.2 49.0 %all-gather.6.cloned.1.call-done = bf16[1,64,128,128]{3,2,0,1:T(8,128)(2,1)} async-done(((bf16[1,8,128,128]{3,2,0,1:T(8,128)(2,1)}), bf16[1,64,128,128]{3,2,0,1:T(8,128)(2,1)}) %all-gather.6.cloned.1.call-update) | async-done | bytes 2097168 | tf_op jit(solution)/shard_map/all_gather | solution.py:75
  291.2 4.6 gather_fusion.4
  295.8 4.5 broadcast_select_fusion
  300.3 6.7 %all-to-all-start.1 = ((bf16[16,1,8,128,128]{4,3,2,1,0:T(8,128)(2,1)}), bf16[16,1,8,128,128]{4,3,2,1,0:T(8,128)(2,1)}, u32[]{:S(2)}, u32[]{:S(2)}) async-start(bf16[16,1,8,128,128]{4,3,2,1,0:T(8,128)(2,1)} %broadcast_select_fusion), calls=%async_computation.2 | async-start | bytes 8388608 | tf_op jit(solution)/shard_map/all_to_all | solution.py:77
  307.0 0.2 reduce-scatter.5.cloned.1.call-start
  307.3 0.3 select_reduce_fusion
  307.8 0.1 reshape.706
  307.9 1.3 gather_fusion.8
  309.2 0.1 reshape.709
  309.2 0.1 fusion.49
  309.3 0.4 fusion.33
  309.7 0.1 broadcast_or_fusion
  309.8 0.1 reshape.653
  309.9 23.3 %gather_fusion.3 = bf16[1024,128,128]{2,1,0:T(8,128)(2,1)} fusion(bf16[16,8,128,128]{3,2,1,0:T(8,128)(2,1)} %param.11, s32[1024]{0:T(1024)S(1)} %reshape.653), kind=kCustom, calls=%fused_computation.5 | custom fusion | bytes 67117056 | tf_op jit(solution)/shard_map/gather | solution.py:42
  333.2 29.6 %all-to-all-done.1 = bf16[16,1,8,128,128]{4,3,2,1,0:T(8,128)(2,1)} async-done(((bf16[16,1,8,128,128]{4,3,2,1,0:T(8,128)(2,1)}), bf16[16,1,8,128,128]{4,3,2,1,0:T(8,128)(2,1)}, u32[]{:S(2)}, u32[]{:S(2)}) %all-to-all-start.1) | async-done | bytes 4194336 | tf_op jit(solution)/shard_map/all_to_all | solution.py:77
  362.8 17.8 %bitcast_convert_fusion = bf16[16,8,128,128]{3,2,1,0:T(8,128)(2,1)} fusion(bf16[16,8,8,128,128]{4,3,2,1,0:T(8,128)(2,1)} %bitcast.162, bf16[16,1,8,128,128]{4,3,2,1,0:T(8,128)(2,1)} %all-to-all-done.1), kind=kOutput, calls=%fused_computation.9 | convolution fusion | flops 4297064448 | bytes 41943040 | tf_op jit(solution)/shard_map/kabij,kbjl->kail/dot_general | solution.py:43
  380.7 0.7 dynamic_slice.23
  383.2 0.1 fusion.63
  383.3 0.9 fusion.22
  384.2 2.0 all-gather.8.cloned.1.call-done
  386.3 2.8 gather_fusion.5
  389.1 0.9 fusion.21
  390.0 84.9 %reduce-scatter.5.cloned.1.call-done = bf16[1,8,128,128]{3,2,1,0:T(8,128)(2,1)} async-done(((bf16[16,8,128,128]{3,2,1,0:T(8,128)(2,1)}), bf16[1,8,128,128]{3,2,1,0:T(8,128)(2,1)}) %reduce-scatter.5.cloned.1.call-update) | async-done | bytes 262160 | tf_op jit(solution)/shard_map/reduce_scatter | solution.py:79
  474.8 1.2 fusion.10
  476.0 0.9 fusion.20
  476.9 0.1 copy.193
  478.3 0.1 copy.201
  479.0 68.4 %all-reduce.6.cloned.1.call-done = (bf16[1,128,128]{1,2,0:T(8,128)(2,1)}, bf16[1,128,128]{2,1,0:T(8,128)(2,1)}, bf16[1,128,128]{1,2,0:T(8,128)(2,1)}) async-done(((bf16[1,128,128]{1,2,0:T(8,128)(2,1)}, bf16[1,128,128]{2,1,0:T(8,128)(2,1)}, bf16[1,128,128]{1,2,0:T(8,128)(2,1)}), (bf16[1,128,128]{1,2,0:T(8,128)(2,1)}, bf16[1,128,128]{2,1,0:T(8,128)(2,1)}, ...) | async-done | bytes 98320 | tf_op jit(solution)/shard_map/psum | solution.py:90
  547.4 0.8 subtract_convert_fusion
  548.2 0.1 copy.203
  548.3 25.1 %all_gather.15 = bf16[16,128,128]{2,1,0:T(8,128)(2,1)S(1)} all-gather(bf16[1,128,128]{2,1,0:T(8,128)(2,1)S(1)} %copy.203), channel_id=1, replica_groups=mesh['prow'=8,'pcol'=16] {'pcol'}, dimensions={0}, use_global_device_ids=true | all-gather | bytes 557056 | tf_op jit(solution)/shard_map/all_gather | solution.py:94
  573.4 0.9 fusion.16
  574.3 1.0 fusion.15
  575.3 0.7 copy.204
  (68 shorter events, 1.4 us)
Async XLA Ops:
  7.2 467.7 %copy-start = (bf16[1,128,128]{2,1,0:T(8,128)(2,1)S(1)}, bf16[1,128,128]{2,1,0:T(8,128)(2,1)}, u32[]{:S(2)}) copy-start(bf16[1,128,128]{2,1,0:T(8,128)(2,1)} %param.18) | copy-start | bytes 98308
  7.2 55.2 %all-gather.4.cloned.1.call-start = ((), (), s32[]{:S(2)}) async-start(), calls=%async_computation.4 | async-start | bytes 2359296 | tf_op jit(solution)/shard_map/all_gather | solution.py:65
  71.6 6.9 %copy-start.11 = (s32[16]{0:T(128)S(1)}, s32[16]{0:T(128)}, u32[]{:S(2)}) copy-start(s32[16]{0:T(128)} %param.15) | copy-start | bytes 196
  71.6 7.0 %copy-start.1 = (s32[16,64]{1,0:T(8,128)S(1)}, s32[16,64]{1,0:T(8,128)}, u32[]{:S(2)}) copy-start(s32[16,64]{1,0:T(8,128)} %param.12) | copy-start | bytes 12292
  71.6 7.5 %copy-start.10 = (s32[16,64]{1,0:T(8,128)S(1)}, s32[16,64]{1,0:T(8,128)}, u32[]{:S(2)}) copy-start(s32[16,64]{1,0:T(8,128)} %param.16) | copy-start | bytes 12292
  71.6 59.8 %all-to-all-start = ((bf16[16,1,8,128,128]{4,3,2,1,0:T(8,128)(2,1)}), bf16[16,1,8,128,128]{4,3,2,1,0:T(8,128)(2,1)}, u32[]{:S(2)}, u32[]{:S(2)}) async-start(bf16[16,1,8,128,128]{4,3,2,1,0:T(8,128)(2,1)} %broadcast_select_fusion.1), calls=%async_computation | async-start | bytes 8388608 | tf_op jit(solution)/shard_map/all_to_all | solution.py:67
  78.5 161.0 %reduce-scatter.3.cloned.1.call-start = ((), (), s32[]{:S(2)}) async-start(), calls=%async_computation.5 | async-start | bytes 4456448 | tf_op jit(solution)/shard_map/reduce_scatter | solution.py:69
  149.1 142.1 %all-gather.6.cloned.1.call-start = ((), (), s32[]{:S(2)}) async-start(), calls=%async_computation.6 | async-start | bytes 2359296 | tf_op jit(solution)/shard_map/all_gather | solution.py:75
  149.8 236.4 %all-gather.8.cloned.1.call-start = ((), (), s32[]{:S(2)}) async-start(), calls=%async_computation.8 | async-start | bytes 4456448 | tf_op jit(solution)/shard_map/all_gather | solution.py:93
  300.3 62.5 %all-to-all-start.1 = ((bf16[16,1,8,128,128]{4,3,2,1,0:T(8,128)(2,1)}), bf16[16,1,8,128,128]{4,3,2,1,0:T(8,128)(2,1)}, u32[]{:S(2)}, u32[]{:S(2)}) async-start(bf16[16,1,8,128,128]{4,3,2,1,0:T(8,128)(2,1)} %broadcast_select_fusion), calls=%async_computation.2 | async-start | bytes 8388608 | tf_op jit(solution)/shard_map/all_to_all | solution.py:77
  307.0 167.8 %reduce-scatter.5.cloned.1.call-start = ((), (), s32[]{:S(2)}) async-start(), calls=%async_computation.7 | async-start | bytes 4456448 | tf_op jit(solution)/shard_map/reduce_scatter | solution.py:79
  380.6 2.7 copy-start.3
  380.6 2.7 copy-start.5
  380.6 8.5 %copy-start.2 = (bf16[1,8,128,128]{3,2,1,0:T(8,128)(2,1)S(1)}, bf16[1,8,128,128]{3,2,1,0:T(8,128)(2,1)}, u32[]{:S(2)}) copy-start(bf16[1,8,128,128]{3,2,1,0:T(8,128)(2,1)} %param.17) | copy-start | bytes 786436
  380.6 96.3 %copy-start.8 = (f32[1,128,128]{2,1,0:T(8,128)S(1)}, f32[1,128,128]{2,1,0:T(8,128)}, u32[]{:S(2)}) copy-start(f32[1,128,128]{2,1,0:T(8,128)} %param.14) | copy-start | bytes 196612
  380.6 97.7 %copy-start.9 = (f32[1,128,128]{2,1,0:T(8,128)S(1)}, f32[1,128,128]{2,1,0:T(8,128)}, u32[]{:S(2)}) copy-start(f32[1,128,128]{2,1,0:T(8,128)} %param.19) | copy-start | bytes 196612
  380.6 166.7 %all-reduce.6.cloned.1.call-start = ((), (), s32[]{:S(2)}) async-start(), calls=%async_computation.9 | async-start | bytes 196608 | tf_op jit(solution)/shard_map/psum | solution.py:90
  476.0 100.0 %copy-start.4 = (bf16[1,8,128,128]{3,2,1,0:T(8,128)(2,1)}, bf16[1,8,128,128]{3,2,1,0:T(8,128)(2,1)S(1)}, u32[]{:S(2)}) copy-start(bf16[1,8,128,128]{3,2,1,0:T(8,128)(2,1)S(1)} %fusion.10) | copy-start | bytes 786436
  548.3 27.7 %copy-start.6 = (bf16[1,128,128]{2,1,0:T(8,128)(2,1)}, bf16[1,128,128]{2,1,0:T(8,128)(2,1)S(1)}, u32[]{:S(2)}) copy-start(bf16[1,128,128]{2,1,0:T(8,128)(2,1)S(1)} %copy.203) | copy-start | bytes 98308
  574.3 1.7 copy-start.7
Sparse Core Ops, SparseCore 0:
  9.6 52.7 all-gather.3
  149.2 90.2 reduce-scatter.2
  241.1 50.0 all-gather.5
  294.1 92.1 all-gather.7
  390.1 84.6 reduce-scatter.4
  477.9 69.4 all-reduce.5
where the time goes:
time: 588 us; the launch traced here: 583 us
  waiting for transfers between devices  395 us (67%)
  local copies, waits for them, and re-layouts  71.9 us (12%)
  matrix products  41.2 us (7%)
  blocking collectives  25.1 us (4%)
  between operations  18.3 us (3%)
  other arithmetic  17 us (3%)
  starting transfers between devices  14 us (2%)
    reduce_scatter x1, waiting for transfers between devices, local(): lax.psum_scatter(tile_products(inverse_top, flat_one, row_one, col_one).a...  89.4 us
    reduce_scatter x1, waiting for transfers between devices, local(): lax.psum_scatter(tile_products(inverse_top, flat_two, row_two, col_two).a...  84.9 us
    psum x1, waiting for transfers between devices, local(): lax.psum(diag_part.astype(jnp.bfloat16), 'prow').astype(jnp.float32)  68.4 us
    all_gather x1, waiting for transfers between devices, local(): full_one = lax.all_gather(panel_one, 'prow', axis=1, tiled=True)  52.6 us
    all_gather x1, waiting for transfers between devices, local(): full_two = lax.all_gather(panel_two, 'prow', axis=1, tiled=True)  49 us
    gather x2, local copies, waits for them, and re-layouts, tile_products(): blocks = inverse_local[row_local[:, :, None], col_local[:, None, :]]  46.6 us
    dot_general x2, matrix products, tile_products(): jnp.einsum('kabij,kbjl->kail', blocks, received, preferred_element_type=j...  35.5 us
    all_to_all x1, waiting for transfers between devices, local(): lax.all_to_all(outgoing_two, 'pcol', split_axis=0, concat_axis=0, tiled=T...  29.6 us
  transfers between devices with their start and end apart: 8, of which 8 were waited for; matrix products, arithmetic and copies ran while one was open for 17% of the time, Pallas kernels for 0%

commit v1 on v0

v1 whole, which is shorter than its diff:
```python
import functools

import jax
import jax.numpy as jnp
from jax import lax
from jax.experimental import pallas as pl
from jax.experimental.pallas import tpu as pltpu
from jax.sharding import PartitionSpec as P

F32 = jnp.float32
BF = jnp.bfloat16
COL = 9


def tdot(a, b):
    return lax.dot_general(a, b, (((0,), (0,)), ((), ())), preferred_element_type=F32)


def kernel(
    rows_ref, parent_ref, order_ref, inv_ref, p1_ref, b1_ref, p2_ref, link_ref, b2_ref,
    c1_ref, d1_ref, c2_ref, u2_ref, d2_ref,
    tf, xb, yp, fb, nb, ys, yr, gz, sc, cc, yb, dd, ar, pv1, pv2, keep, snd, rcv, loc,
):
    tl = inv_ref.shape[-1]
    p = lax.axis_index("prow")
    c = lax.axis_index("pcol")
    x, yl = p // 2, p % 2
    yh, j, z, q = c // 8, c // 2, (c // 2) % 4, c % 2
    xl, xr, xo = (x + 3) % 4, (x + 1) % 4, (x + 2) % 4
    zl, zr, zo = (z + 3) % 4, (z + 1) % 4, (z + 2) % 4

    left_x = (2 * xl + yl, c)
    right_x = (2 * xr + yl, c)
    mate_y = (2 * x + 1 - yl, c)
    left_z = (p, 8 * yh + 2 * zl + q)
    right_z = (p, 8 * yh + 2 * zr + q)
    core = (p, 2 * j + 1 - q)
    far_y = (p, 8 * (1 - yh) + 2 * z + q)
    turned = (j, 2 * p + q)


    def remote(src, dst, at, to, send_at=None):
        return pltpu.make_async_remote_copy(
            src_ref=src, dst_ref=dst, send_sem=snd.at[at if send_at is None else send_at], recv_sem=rcv.at[at],
            device_id=to, device_id_type=pl.DeviceIdType.MESH)

    T_AT = 0
    X_AT = 1
    XS_AT = 17
    FAR_AT = 21
    NE_AT = 29
    NL_AT = 37
    Y_AT = 45
    G_AT = 47
    C_AT = 51
    D_AT = 52
    A_AT = 53
    panels = (p1_ref, p2_ref)

    slots = (p, 2 * x + 1 - yl, 2 * xl + yl, 2 * xr + yl, 2 * xl + 1 - yl, 2 * xr + 1 - yl, 2 * xo + yl, 2 * xo + 1 - yl)

    def turn(l):
        return remote(panels[l].at[0], xb.at[l, j], X_AT + 8 * l, turned)

    def turn_here(l):
        return pltpu.make_async_copy(panels[l].at[0], xb.at[l, p], loc.at[l])

    def send_y(l):
        return remote(xb.at[l, p], xb.at[l, p], X_AT + 8 * l + 1, mate_y)

    def send_x(l, which, to_right):
        s = slots[which]
        at = X_AT + 8 * l + 2 + 2 * which + (0 if to_right else 1)
        return remote(xb.at[l, s], xb.at[l, s], at, right_x if to_right else left_x)

    def forward(l, which, to_right):
        s = slots[2 + 2 * which + (0 if to_right else 1)]
        part = pl.ds(0, 4) if to_right else pl.ds(4, 4)
        at = X_AT + 8 * l + 6 + which
        sat = at if to_right else XS_AT + 2 * l + which
        return remote(xb.at[l, s, part], xb.at[l, s, part], at, right_x if to_right else left_x, sat)

    def arrived(l, i):
        s = slots[i]
        return remote(xb.at[l, s], xb.at[l, s], X_AT + 8 * l + i, right_x)

    def far(l, yd, dr):
        h = 4 * yd + zo
        part = pl.ds(4 * dr, 4)
        return remote(yp.at[l, h, part], fb.at[l, yd, dr], FAR_AT + 4 * l + 2 * yd + dr, (right_z, left_z)[dr])

    def near_early(l, yd, dr):
        h = 4 * yd + (zr, zl)[dr]
        part = pl.ds(4 - 4 * dr, 4)
        return remote(yp.at[l, h, part], nb.at[l, yd, dr, part], NE_AT + 4 * l + 2 * yd + dr, (right_z, left_z)[dr])

    def near_late(l, yd, dr):
        h = 4 * yd + (zr, zl)[dr]
        part = pl.ds(4 * dr, 4)
        return remote(yp.at[l, h, part], nb.at[l, yd, dr, part], NL_AT + 4 * l + 2 * yd + dr, (right_z, left_z)[dr])

    def across(l):
        return remote(ys.at[l], yr.at[l], Y_AT + l, far_y)

    t_here = pltpu.make_async_copy(inv_ref, tf.at[q], loc.at[2])
    t_here.start()
    v1 = pltpu.make_async_copy(p1_ref.at[0], pv1, loc.at[3])
    v2 = pltpu.make_async_copy(p2_ref.at[0], pv2, loc.at[4])
    v1.start()
    v2.start()

    barrier = pltpu.get_barrier_semaphore()

    def greet(to):
        pl.semaphore_signal(barrier, inc=1, device_id=to, device_id_type=pl.DeviceIdType.MESH)

    for d in range(1, 8):
        greet(((p + d) % 8, c))
    for to in (left_z, right_z, core, far_y):
        greet(to)

    @pl.when(p != j)
    def _():
        greet(turned)
        pl.semaphore_wait(barrier, 12)

    @pl.when(p == j)
    def _():
        pl.semaphore_wait(barrier, 11)

    def start_turn(l):
        @pl.when(p != j)
        def _():
            turn(l).start()

        @pl.when(p == j)
        def _():
            turn_here(l).start()

    def wait_turn(l):
        @pl.when(p != j)
        def _():
            arrived(l, 0).wait_recv()

        @pl.when(p == j)
        def _():
            turn_here(l).wait()

    sent = []

    def go(copy):
        copy.start()
        sent.append(copy)

    def own_out(l):
        go(send_y(l))
        go(send_x(l, 0, True))
        go(send_x(l, 0, False))

    def mate_out(l):
        arrived(l, 1).wait_recv()
        go(send_x(l, 1, True))
        go(send_x(l, 1, False))

    def relay(l, which):
        arrived(l, 2 + 2 * which).wait_recv()
        go(forward(l, which, True))
        arrived(l, 3 + 2 * which).wait_recv()
        go(forward(l, which, False))

    def row_at(l, k, i):
        if l == 0:
            return rows_ref[k, i]
        return rows_ref[parent_ref[k], order_ref[k, i]]

    def products(l, i):
        h = slots[i]
        k = 2 * h + q
        cols = [row_at(l, k, 8 * j + n) for n in range(8)]
        cols = [((a >> 3) & 1, a & 7) for a in cols]

        def one(m, carry):
            r = row_at(l, k, 8 * p + m) & 15
            wide = jnp.concatenate([tf[a, r, b] for a, b in cols], axis=1)
            tall = xb[l, h].reshape(8 * tl, tl)
            yp[l, h, m] = jnp.dot(wide, tall, preferred_element_type=F32).astype(BF)
            return carry

        lax.fori_loop(0, 8, one, 0)
        yd, d = h // 4, (h % 4 + 4 - z) % 4

        @pl.when(d == 2)
        def _():
            far(l, yd, 0).start()
            far(l, yd, 1).start()

        @pl.when(d == 1)
        def _():
            near_early(l, yd, 0).start()

        @pl.when(d == 3)
        def _():
            near_early(l, yd, 1).start()

    def pass_on(l):
        for yd in range(2):
            for dr in range(2):
                far(l, yd, dr).wait_recv()
                h = 4 * yd + (zr, zl)[dr]
                part = pl.ds(4 * dr, 4)
                yp[l, h, part] = (yp[l, h, part].astype(F32) + fb[l, yd, dr].astype(F32)).astype(BF)
                go(near_late(l, yd, dr))

    def meet(l):
        for yd in range(2):
            for dr in range(2):
                near_early(l, yd, dr).wait_recv()
                near_late(l, yd, dr).wait_recv()

        def total(yd, m):
            h = 4 * yd + z
            return yp[l, h, m].astype(F32) + nb[l, yd, 0, m].astype(F32) + nb[l, yd, 1, m].astype(F32)

        for m in range(8):
            ys[l, m] = total(1 - yh, m).astype(BF)
        go(across(l))
        for m in range(8):
            keep[l, m] = total(yh, m)

    def spread(t):
        copies = [
            remote(ar.at[t, p], ar.at[t, p], A_AT + t, ((p + d) % 8, c)) for d in range(1, 8)
        ]
        for copy in copies:
            copy.start()

    def spread_all(t):
        return remote(ar.at[t, pl.ds(0, 7)], ar.at[t, pl.ds(0, 7)], A_AT + t, right_x)

    def spread_sum(t):
        spread_all(t).wait_recv()
        total = ar[t, 0].astype(F32)
        for i in range(1, 8):
            total = total + ar[t, i].astype(F32)
        return total

    start_turn(0)
    t_there = remote(inv_ref, tf.at[q], T_AT, core)
    t_there.start()
    sent.append(t_there)
    wait_turn(0)
    own_out(0)
    start_turn(1)
    mate_out(0)
    t_here.wait()
    t_there.wait_recv()
    products(0, 0)
    products(0, 1)
    relay(0, 0)
    products(0, 2)
    products(0, 3)
    relay(0, 1)
    wait_turn(1)
    own_out(1)
    products(0, 4)
    products(0, 5)
    mate_out(1)
    arrived(0, 6).wait_recv()
    products(0, 6)
    arrived(0, 7).wait_recv()
    products(0, 7)
    pass_on(0)
    products(1, 0)
    products(1, 1)
    relay(1, 0)
    products(1, 2)
    products(1, 3)
    meet(0)
    relay(1, 1)
    products(1, 4)
    products(1, 5)
    v1.wait()
    v2.wait()

    across(0).wait_recv()
    for m in range(8):
        tile = (-(keep[0, m] + yr[0, m].astype(F32))).astype(BF)
        c1_ref[0, m] = tile
        gz[z, m] = tile
    share = tdot(pv1[...].reshape(8 * tl, tl), c1_ref[0].reshape(8 * tl, tl))
    ar[0, p] = share.astype(BF)
    spread(0)
    first = jnp.where(p == 0, 1.0, 0.0).astype(F32)
    gz[z, 8] = (b1_ref[0] * first - share).astype(BF)
    g_right = remote(gz.at[z], gz.at[z], G_AT, right_z)
    g_left = remote(gz.at[z], gz.at[z], G_AT + 1, left_z)
    go(g_right)
    go(g_left)

    arrived(1, 6).wait_recv()
    products(1, 6)
    arrived(1, 7).wait_recv()
    products(1, 7)
    pass_on(1)

    remote(gz.at[zl], gz.at[zl], G_AT, right_z).wait_recv()
    go(remote(gz.at[zl, pl.ds(0, 5)], gz.at[zl, pl.ds(0, 5)], G_AT + 2, right_z))
    remote(gz.at[zr], gz.at[zr], G_AT + 1, right_z).wait_recv()
    go(remote(gz.at[zr, pl.ds(5, 4)], gz.at[zr, pl.ds(5, 4)], G_AT + 2, left_z, G_AT + 3))

    d1_ref[0] = (b1_ref[0] - spread_sum(0)).astype(BF)

    remote(gz.at[zo], gz.at[zo], G_AT + 2, right_z).wait_recv()
    for yd in range(2):
        there = parent_ref[8 * yd + 2 * z + 1 - q]
        sc[yd] = gz[(there >> 1) & 3]
    to_core = remote(sc, cc.at[q], C_AT, core)
    go(to_core)
    for yd in range(2):
        here = parent_ref[8 * yd + 2 * z + q]
        cc[q, yd] = gz[(here >> 1) & 3]
    meet(1)
    to_core.wait_recv()
    yb[...] = cc[parent_ref[8 * (1 - yh) + 2 * z + q] & 1, 1 - yh]
    to_far = remote(yb, dd.at[yh], D_AT, far_y)
    go(to_far)
    mine = parent_ref[c]
    dd[yh] = cc[mine & 1, yh]
    to_far.wait_recv()

    link = link_ref[0]
    around = (mine >> 3) & 1
    near = [dd[around, order_ref[c, 8 * p + m] & 7] for m in range(8)]
    near_all = jnp.concatenate(near, axis=0)
    upper = tdot(near_all, pv2[...].reshape(8 * tl, tl)) + jnp.dot(dd[around, 8], link, preferred_element_type=F32)
    ar[1, p] = upper.astype(BF)
    spread(1)
    for m in range(8):
        keep[1, m] = keep[1, m] + jnp.dot(near[m], link, preferred_element_type=F32)
    across(1).wait_recv()
    for m in range(8):
        c2_ref[0, m] = (-(keep[1, m] + yr[1, m].astype(F32))).astype(BF)
    lower = tdot(pv2[...].reshape(8 * tl, tl), c2_ref[0].reshape(8 * tl, tl))
    ar[2, p] = lower.astype(BF)
    spread(2)
    u2 = (-spread_sum(1)).astype(BF)
    u2_ref[0] = u2
    rest = b2_ref[0] - tdot(link, u2)
    d2_ref[0] = (rest - spread_sum(2)).astype(BF)

    for copy in sent:
        copy.wait_send()
    for l in range(2):
        @pl.when(p != j)
        def _():
            turn(l).wait_send()

        for yd in range(2):
            for dr in range(2):
                far(l, yd, dr).wait_send()
                near_early(l, yd, dr).wait_send()
    for t in range(3):
        spread_all(t).wait_send()


def local(inverse_top, rows_one, panel_one, base_one, parent_two, order_two, panel_two, link_two, base_two):
    tl = inverse_top.shape[-1]
    vm = lambda *s: pltpu.VMEM(s + (tl, tl), BF)
    anyw = pl.BlockSpec(memory_space=pl.ANY)
    smem = pl.BlockSpec(memory_space=pltpu.SMEM)
    vmem = pl.BlockSpec(memory_space=pltpu.VMEM)
    one = jax.ShapeDtypeStruct(panel_one.shape, BF)
    tile = jax.ShapeDtypeStruct(link_two.shape, BF)
    return pl.pallas_call(
        kernel,
        out_shape=(one, tile, one, tile, tile),
        in_specs=[smem, smem, smem, anyw, anyw, vmem, anyw, vmem, vmem],
        out_specs=[vmem] * 5,
        scratch_shapes=[
            vm(2, 16, 8), vm(2, 8, 8), vm(2, 8, 8),
            vm(2, 2, 2, 4), vm(2, 2, 2, 8), vm(2, 8), vm(2, 8),
            vm(4, COL), vm(2, COL), vm(2, 2, COL), vm(COL), vm(2, COL), vm(3, 8),
            vm(8), vm(8), pltpu.VMEM((2, 8, tl, tl), F32),
            pltpu.SemaphoreType.DMA((56,)), pltpu.SemaphoreType.DMA((56,)), pltpu.SemaphoreType.DMA((5,)),
        ],
        compiler_params=pltpu.CompilerParams(
            collective_id=0, has_side_effects=True, vmem_limit_bytes=56 * 1024 * 1024),
    )(rows_one, parent_two, order_two, inverse_top, panel_one, base_one, panel_two, link_two, base_two)


def solution(mesh):
    return jax.shard_map(
        local,
        mesh=mesh,
        in_specs=(
            P("prow", "pcol", None, None), P(), P("pcol", "prow", None, None), P("pcol", None, None), P(),
            P(), P("pcol", "prow", None, None), P("pcol", None, None), P("pcol", None, None),
        ),
        out_specs=(
            P("pcol", "prow", None, None), P("pcol", None, None), P("pcol", "prow", None, None),
            P("pcol", None, None), P("pcol", None, None),
        ),
        check_vma=False,
    )
```

time: 588 us -> 145 us (0.25)
  waiting for transfers between devices: 395 us -> 0 us
  Pallas kernels: 0 us -> 136 us
  local copies, waits for them, and re-layouts: 71.9 us -> 7.46 us
  matrix products: 41.2 us -> 0 us
  blocking collectives: 25.1 us -> 0 us
  between operations: 18.3 us -> 0.64 us
  other arithmetic: 17 us -> 0 us
  starting transfers between devices: 14 us -> 0 us
    reduce_scatter x2 -> x0, waiting for transfers between devices: 174 us -> none  [the longest x1 89.4 us: local(): lax.psum_scatter(tile_products(inverse_top, flat_one, row_one, col_one).a...]
    pallas_call x0 -> x1, Pallas kernels: none -> 136 us  [local(): pl.pallas_call(kernel, out_shape=(one, tile, one, tile, tile), in_specs=[...]
    all_gather x3 -> x0, waiting for transfers between devices: 104 us -> none  [the longest x1 52.6 us: local(): full_one = lax.all_gather(panel_one, 'prow', axis=1, tiled=True)]
    gather x19 -> x0, local copies, waits for them, and re-layouts: 69.5 us -> none  [the longest x2 46.6 us: tile_products(): blocks = inverse_local[row_local[:, :, None], col_local[:, None, :]]]
    psum x1 -> x0, waiting for transfers between devices: 68.4 us -> none  [local(): lax.psum(diag_part.astype(jnp.bfloat16), 'prow').astype(jnp.float32)]
    all_to_all x2 -> x0, waiting for transfers between devices: 47.7 us -> none  [the longest x1 29.6 us: local(): lax.all_to_all(outgoing_two, 'pcol', split_axis=0, concat_axis=0, tiled=T...]
    dot_general x8 -> x0, matrix products: 41.2 us -> none  [the longest x2 35.5 us: tile_products(): jnp.einsum('kabij,kbjl->kail', blocks, received, preferred_element_type=j...]
    all_gather x1 -> x0, blocking collectives: 25.1 us -> none  [local(): lax.all_gather(diagonal_one, 'pcol', axis=0, tiled=True)]
  transfers between devices with their start and end apart: 8 -> 0, of which waited for: 8 -> 0; matrix products, arithmetic and copies ran while one was open for 17% -> 0% of each run, Pallas kernels for 0% -> 0%
where the time goes in v1:
time: 145 us; the launch traced here: 144 us
  Pallas kernels  136 us (94%)
  local copies, waits for them, and re-layouts  7.46 us (5%)
    pallas_call x1, Pallas kernels, local(): pl.pallas_call(kernel, out_shape=(one, tile, one, tile, tile), in_specs=[...  136 us
    unnamed x5, local copies, waits for them, and re-layouts  7.46 us

profile of v1, /device:TPU:8, one launch (start us, length us, event | category | flops | bytes accessed | tf_op | source)
XLA Modules:
  0.0 144.5 jit_solution(6664720107919834983)
XLA Ops:
  0.6 136.4 %shard_map.128 = (bf16[1,8,128,128]{3,2,1,0:T(8,128)(2,1)}, bf16[1,128,128]{2,1,0:T(8,128)(2,1)}, bf16[1,8,128,128]{3,2,1,0:T(8,128)(2,1)}, bf16[1,128,128]{2,1,0:T(8,128)(2,1)}, bf16[1,128,128]{2,1,0:T(8,128)(2,1)}) custom-call(s32[16,64]{1,0:T(8,128)} %rows_ref.1, s32[16]{0:T(128)} %parent_ref.1, s32[16,64]{1,0:T(8,128)} %order_ref.1, ...), custom_call_target="tpu_custom_call" | custom-call | tf_op jit(solution)/shard_map/pallas_call | solution.py:374
  137.0 1.7 %copy.19 = bf16[1,8,128,128]{3,2,1,0:T(8,128)(2,1)} copy(bf16[1,8,128,128]{3,2,1,0:T(8,128)(2,1)} %get-tuple-element.10) | data formatting | bytes 524288
  138.7 1.4 copy.20
  140.1 1.7 %copy.21 = bf16[1,8,128,128]{3,2,1,0:T(8,128)(2,1)} copy(bf16[1,8,128,128]{3,2,1,0:T(8,128)(2,1)} %get-tuple-element.12) | data formatting | bytes 524288
  141.7 1.4 copy.22
  143.1 1.4 copy.23

commit v2 on v1

v2 whole, which is shorter than its diff:
```python
import functools

import jax
import jax.numpy as jnp
from jax import lax
from jax.experimental import pallas as pl
from jax.experimental.pallas import tpu as pltpu
from jax.sharding import PartitionSpec as P

F32 = jnp.float32
BF = jnp.bfloat16
COL = 9


def tdot(a, b):
    return lax.dot_general(a, b, (((0,), (0,)), ((), ())), preferred_element_type=F32)


def kernel(
    rows_ref, parent_ref, order_ref, inv_ref, p1_ref, b1_ref, p2_ref, link_ref, b2_ref,
    out_ref,
    tf, xb, yp, fb, nb, ys, yr, gz, sc, cc, yb, dd, ar, pv1, pv2, keep, snd, rcv, loc,
):
    tl = inv_ref.shape[-1]
    p = lax.axis_index("prow")
    c = lax.axis_index("pcol")
    x, yl = p // 2, p % 2
    yh, j, z, q = c // 8, c // 2, (c // 2) % 4, c % 2
    xl, xr, xo = (x + 3) % 4, (x + 1) % 4, (x + 2) % 4
    zl, zr, zo = (z + 3) % 4, (z + 1) % 4, (z + 2) % 4

    left_x = (2 * xl + yl, c)
    right_x = (2 * xr + yl, c)
    mate_y = (2 * x + 1 - yl, c)
    left_z = (p, 8 * yh + 2 * zl + q)
    right_z = (p, 8 * yh + 2 * zr + q)
    core = (p, 2 * j + 1 - q)
    far_y = (p, 8 * (1 - yh) + 2 * z + q)

    def held(slot):
        return 4 * (slot % 2) + (slot // 2 + z) % 4

    to_p = 2 * ((z + 4 - p % 4) % 4) + yh
    turned = (to_p, 2 * p + q)
    source = (j, 2 * held(p) + q)
    stays = jnp.logical_and(to_p == p, c == 2 * p + q)

    parity = (yl, 1 - yl, 1 - yh, yh)
    level = (0, 0, 1, 1)

    def slot(t, xs):
        return 2 * xs + parity[t]

    def remote(src, dst, at, to, send_at=None):
        return pltpu.make_async_remote_copy(
            src_ref=src, dst_ref=dst, send_sem=snd.at[at if send_at is None else send_at], recv_sem=rcv.at[at],
            device_id=to, device_id_type=pl.DeviceIdType.MESH)

    T_AT, TURN_AT, MATE_AT, BASE_AT, FWD_AT, FWD_LEFT_AT = 0, 1, 3, 5, 13, 17
    FAR_AT, NE_AT, NL_AT, Y_AT, G_AT, C_AT, D_AT, A_AT = 21, 29, 37, 45, 47, 51, 52, 53
    panels = (p1_ref, p2_ref)

    def turn(l):
        return remote(panels[l].at[0], xb.at[l, to_p], TURN_AT + l, turned)

    def turn_here(l):
        return pltpu.make_async_copy(panels[l].at[0], xb.at[l, p], loc.at[l])

    def mate(l):
        return remote(xb.at[l, p], xb.at[l, p], MATE_AT + l, mate_y)

    def base(t, dr):
        at = xb.at[level[t], slot(t, x)]
        return remote(at, at, BASE_AT + 2 * t + dr, (right_x, left_x)[dr])

    def base_in(t, dr):
        at = xb.at[level[t], slot(t, (xl, xr)[dr])]
        return remote(at, at, BASE_AT + 2 * t + dr, right_x)

    def forward(t, dr):
        at = xb.at[level[t], slot(t, (xl, xr)[dr]), pl.ds(4 * dr, 4)]
        return remote(at, at, FWD_AT + t, (right_x, left_x)[dr], (FWD_AT, FWD_LEFT_AT)[dr] + t)

    def forward_in(t):
        at = xb.at[level[t], slot(t, xo)]
        return remote(at, at, FWD_AT + t, right_x)

    def far(t, dr):
        return remote(yp.at[t, zo, pl.ds(4 * dr, 4)], fb.at[t, dr], FAR_AT + 2 * t + dr, (right_z, left_z)[dr])

    def near_early(t, dr):
        part = pl.ds(4 - 4 * dr, 4)
        return remote(yp.at[t, (zr, zl)[dr], part], nb.at[t, dr, part], NE_AT + 2 * t + dr, (right_z, left_z)[dr])

    def near_late(t, dr):
        part = pl.ds(4 * dr, 4)
        return remote(yp.at[t, (zr, zl)[dr], part], nb.at[t, dr, part], NL_AT + 2 * t + dr, (right_z, left_z)[dr])

    def across(l):
        return remote(ys.at[l], yr.at[l], Y_AT + l, far_y)

    t_here = pltpu.make_async_copy(inv_ref, tf.at[q], loc.at[2])
    t_here.start()
    v1 = pltpu.make_async_copy(p1_ref.at[0], pv1, loc.at[3])
    v2 = pltpu.make_async_copy(p2_ref.at[0], pv2, loc.at[4])
    v1.start()
    v2.start()

    barrier = pltpu.get_barrier_semaphore()

    def greet(to):
        pl.semaphore_signal(barrier, inc=1, device_id=to, device_id_type=pl.DeviceIdType.MESH)

    @pl.when(jnp.logical_not(stays))
    def _():
        greet(source)

    for d in range(1, 8):
        greet(((p + d) % 8, c))
    for to in (left_z, right_z, core, far_y):
        greet(to)

    @pl.when(jnp.logical_not(stays))
    def _():
        pl.semaphore_wait(barrier, 12)

    @pl.when(stays)
    def _():
        pl.semaphore_wait(barrier, 11)

    def start_turn(l):
        @pl.when(jnp.logical_not(stays))
        def _():
            turn(l).start()

        @pl.when(stays)
        def _():
            turn_here(l).start()

    def wait_turn(l):
        @pl.when(jnp.logical_not(stays))
        def _():
            remote(xb.at[l, p], xb.at[l, p], TURN_AT + l, right_x).wait_recv()

        @pl.when(stays)
        def _():
            turn_here(l).wait()

    sent = []

    def go(copy):
        copy.start()
        sent.append(copy)

    def wait_mate(l):
        s = 2 * x + 1 - yl
        remote(xb.at[l, s], xb.at[l, s], MATE_AT + l, right_x).wait_recv()

    def base_out(t):
        go(base(t, 0))
        go(base(t, 1))

    def relay(t):
        for dr in range(2):
            base_in(t, dr).wait_recv()
            go(forward(t, dr))

    def row_at(l, k, i):
        if l == 0:
            return rows_ref[k, i]
        return rows_ref[parent_ref[k], order_ref[k, i]]

    def products(t, xs):
        l, s, zh = level[t], slot(t, xs), (xs + z) % 4
        k = 2 * held(s) + q
        cols = [row_at(l, k, 8 * j + n) for n in range(8)]
        cols = [((a >> 3) & 1, a & 7) for a in cols]

        def one(m, carry):
            r = row_at(l, k, 8 * p + m) & 15
            wide = jnp.concatenate([tf[a, r, b] for a, b in cols], axis=1)
            tall = xb[l, s].reshape(8 * tl, tl)
            yp[t, zh, m] = jnp.dot(wide, tall, preferred_element_type=F32).astype(BF)
            return carry

        lax.fori_loop(0, 8, one, 0)

        @pl.when(xs == 2)
        def _():
            far(t, 0).start()
            far(t, 1).start()

        @pl.when(xs == 1)
        def _():
            near_early(t, 0).start()

        @pl.when(xs == 3)
        def _():
            near_early(t, 1).start()

    def pass_on(t):
        for dr in range(2):
            far(t, dr).wait_recv()
            zh, part = (zr, zl)[dr], pl.ds(4 * dr, 4)
            yp[t, zh, part] = (yp[t, zh, part].astype(F32) + fb[t, dr].astype(F32)).astype(BF)
            go(near_late(t, dr))

    def meet(t):
        l = level[t]
        for dr in range(2):
            near_early(t, dr).wait_recv()
            near_late(t, dr).wait_recv()

        def total(m):
            return yp[t, z, m].astype(F32) + nb[t, 0, m].astype(F32) + nb[t, 1, m].astype(F32)

        def cross():
            for m in range(8):
                ys[l, m] = total(m).astype(BF)
            across(l).start()

        def stay():
            for m in range(8):
                keep[l, m] = total(m)

        if t == 2:
            cross()
        elif t == 3:
            stay()
        else:
            pl.when(parity[t] != yh)(cross)
            pl.when(parity[t] == yh)(stay)

    def spread(t):
        for d in range(1, 8):
            remote(ar.at[t, p], ar.at[t, p], A_AT + t, ((p + d) % 8, c)).start()

    def spread_all(t):
        return remote(ar.at[t, pl.ds(0, 7)], ar.at[t, pl.ds(0, 7)], A_AT + t, right_x)

    def spread_sum(t):
        spread_all(t).wait_recv()
        total = ar[t, 0].astype(F32)
        for i in range(1, 8):
            total = total + ar[t, i].astype(F32)
        return total

    start_turn(0)
    t_there = remote(inv_ref, tf.at[q], T_AT, core)
    go(t_there)
    wait_turn(0)
    go(mate(0))
    base_out(0)
    start_turn(1)
    t_here.wait()
    t_there.wait_recv()
    products(0, x)
    wait_mate(0)
    base_out(1)
    relay(0)
    products(1, x)
    products(0, xl)
    products(0, xr)
    wait_turn(1)
    go(mate(1))
    forward_in(0).wait_recv()
    products(0, xo)
    wait_mate(1)
    base_out(2)
    relay(1)
    products(1, xl)
    products(1, xr)
    pass_on(0)
    base_out(3)
    forward_in(1).wait_recv()
    products(1, xo)
    relay(2)
    products(2, x)
    meet(0)
    pass_on(1)
    products(3, x)
    products(2, xl)
    products(2, xr)
    meet(1)
    relay(3)
    forward_in(2).wait_recv()
    products(2, xo)
    v1.wait()
    v2.wait()

    across(0).wait_recv()
    for m in range(8):
        tile = (-(keep[0, m] + yr[0, m].astype(F32))).astype(BF)
        out_ref[m] = tile
        gz[z, m] = tile
    share = tdot(pv1[...].reshape(8 * tl, tl), gz[z, pl.ds(0, 8)].reshape(8 * tl, tl))
    ar[0, p] = share.astype(BF)
    first = jnp.where(p == 0, 1.0, 0.0).astype(F32)
    gz[z, 8] = (b1_ref[0] * first - share).astype(BF)
    g_right = remote(gz.at[z], gz.at[z], G_AT, right_z)
    g_left = remote(gz.at[z], gz.at[z], G_AT + 1, left_z)
    go(g_right)
    go(g_left)
    spread(0)

    pass_on(2)
    products(3, xl)
    products(3, xr)
    forward_in(3).wait_recv()
    products(3, xo)
    pass_on(3)
    meet(2)

    remote(gz.at[zl], gz.at[zl], G_AT, right_z).wait_recv()
    go(remote(gz.at[zl, pl.ds(0, 5)], gz.at[zl, pl.ds(0, 5)], G_AT + 2, right_z))
    remote(gz.at[zr], gz.at[zr], G_AT + 1, right_z).wait_recv()
    go(remote(gz.at[zr, pl.ds(5, 4)], gz.at[zr, pl.ds(5, 4)], G_AT + 2, left_z, G_AT + 3))

    out_ref[16] = (b1_ref[0] - spread_sum(0)).astype(BF)

    remote(gz.at[zo], gz.at[zo], G_AT + 2, right_z).wait_recv()
    for yd in range(2):
        there = parent_ref[8 * yd + 2 * z + 1 - q]
        sc[yd] = gz[(there >> 1) & 3]
    to_core = remote(sc, cc.at[q], C_AT, core)
    go(to_core)
    for yd in range(2):
        here = parent_ref[8 * yd + 2 * z + q]
        cc[q, yd] = gz[(here >> 1) & 3]
    to_core.wait_recv()
    yb[...] = cc[parent_ref[8 * (1 - yh) + 2 * z + q] & 1, 1 - yh]
    to_far = remote(yb, dd.at[yh], D_AT, far_y)
    go(to_far)
    mine = parent_ref[c]
    dd[yh] = cc[mine & 1, yh]
    meet(3)
    to_far.wait_recv()

    link = link_ref[0]
    around = (mine >> 3) & 1
    near = [dd[around, order_ref[c, 8 * p + m] & 7] for m in range(8)]
    near_all = jnp.concatenate(near, axis=0)
    upper = tdot(near_all, pv2[...].reshape(8 * tl, tl)) + jnp.dot(dd[around, 8], link, preferred_element_type=F32)
    ar[1, p] = upper.astype(BF)
    spread(1)
    for m in range(8):
        keep[1, m] = keep[1, m] + jnp.dot(near[m], link, preferred_element_type=F32)
    across(1).wait_recv()
    for m in range(8):
        out_ref[8 + m] = (-(keep[1, m] + yr[1, m].astype(F32))).astype(BF)
    lower = tdot(pv2[...].reshape(8 * tl, tl), out_ref[pl.ds(8, 8)].reshape(8 * tl, tl))
    ar[2, p] = lower.astype(BF)
    spread(2)
    u2 = (-spread_sum(1)).astype(BF)
    out_ref[17] = u2
    rest = b2_ref[0] - tdot(link, u2)
    out_ref[18] = (rest - spread_sum(2)).astype(BF)

    for copy in sent:
        copy.wait_send()
    for l in range(2):
        @pl.when(jnp.logical_not(stays))
        def _():
            turn(l).wait_send()

        across(l).wait_send()
    for t in range(4):
        for dr in range(2):
            far(t, dr).wait_send()
            near_early(t, dr).wait_send()
    for t in range(3):
        spread_all(t).wait_send()


def unpack(all_ref, c1_ref, d1_ref, c2_ref, u2_ref, d2_ref):
    c1_ref[0] = all_ref[pl.ds(0, 8)]
    c2_ref[0] = all_ref[pl.ds(8, 8)]
    d1_ref[0] = all_ref[16]
    u2_ref[0] = all_ref[17]
    d2_ref[0] = all_ref[18]


def local(inverse_top, rows_one, panel_one, base_one, parent_two, order_two, panel_two, link_two, base_two):
    tl = inverse_top.shape[-1]
    vm = lambda *s: pltpu.VMEM(s + (tl, tl), BF)
    anyw = pl.BlockSpec(memory_space=pl.ANY)
    smem = pl.BlockSpec(memory_space=pltpu.SMEM)
    vmem = pl.BlockSpec(memory_space=pltpu.VMEM)
    one = jax.ShapeDtypeStruct(panel_one.shape, BF)
    tile = jax.ShapeDtypeStruct(link_two.shape, BF)
    packed = pl.pallas_call(
        kernel,
        out_shape=jax.ShapeDtypeStruct((19, tl, tl), BF),
        in_specs=[smem, smem, smem, anyw, anyw, vmem, anyw, vmem, vmem],
        out_specs=vmem,
        scratch_shapes=[
            vm(2, 16, 8), vm(2, 8, 8), vm(4, 4, 8),
            vm(4, 2, 4), vm(4, 2, 8), vm(2, 8), vm(2, 8),
            vm(4, COL), vm(2, COL), vm(2, 2, COL), vm(COL), vm(2, COL), vm(3, 8),
            vm(8), vm(8), pltpu.VMEM((2, 8, tl, tl), F32),
            pltpu.SemaphoreType.DMA((56,)), pltpu.SemaphoreType.DMA((56,)), pltpu.SemaphoreType.DMA((5,)),
        ],
        compiler_params=pltpu.CompilerParams(
            collective_id=0, has_side_effects=True, vmem_limit_bytes=56 * 1024 * 1024),
    )(rows_one, parent_two, order_two, inverse_top, panel_one, base_one, panel_two, link_two, base_two)
    return pl.pallas_call(
        unpack, out_shape=(one, tile, one, tile, tile), in_specs=[vmem], out_specs=[vmem] * 5)(packed)


def solution(mesh):
    return jax.shard_map(
        local,
        mesh=mesh,
        in_specs=(
            P("prow", "pcol", None, None), P(), P("pcol", "prow", None, None), P("pcol", None, None), P(),
            P(), P("pcol", "prow", None, None), P("pcol", None, None), P("pcol", None, None),
        ),
        out_specs=(
            P("pcol", "prow", None, None), P("pcol", None, None), P("pcol", "prow", None, None),
            P("pcol", None, None), P("pcol", None, None),
        ),
        check_vma=False,
    )
```

time: 145 us -> 117 us (0.81)
  the two profiles are of different devices: /device:TPU:8 before, /device:TPU:53 now
where the time goes in v2:
time: 117 us
  Pallas kernels  116 us (99%)
    pallas_call x1, Pallas kernels, local(): pl.pallas_call(kernel, out_shape=jax.ShapeDtypeStruct((19, tl, tl), BF),...  114 us

profile of v2, /device:TPU:53, one launch (start us, length us, event | category | flops | bytes accessed | tf_op | source)
XLA Modules:
  0.0 116.9 jit_solution(1774279909656019419)
XLA Ops:
  0.6 114.4 %shard_map.128.all_ref = bf16[19,128,128]{2,1,0:T(8,128)(2,1)} custom-call(s32[16,64]{1,0:T(8,128)} %rows_ref.1, s32[16]{0:T(128)} %parent_ref.1, s32[16,64]{1,0:T(8,128)} %order_ref.1, bf16[16,8,128,128]{3,2,1,0:T(8,128)(2,1)} %inv_ref.1, bf16[1,8,128,128]{3,2,1,0:T(8,128)(2,1)} %p1_ref.1, f32[1,128,128]{2,1,0:T(8,128)} %b1_ref.1, ...), custom_call_target="tpu_custom_call" | custom-call | tf_op jit(solution)/shard_map/pallas_call | solution.py:391
  115.0 1.9 %shard_map.129 = (bf16[1,8,128,128]{3,2,1,0:T(8,128)(2,1)}, bf16[1,128,128]{2,1,0:T(8,128)(2,1)}, bf16[1,8,128,128]{3,2,1,0:T(8,128)(2,1)}, bf16[1,128,128]{2,1,0:T(8,128)(2,1)}, bf16[1,128,128]{2,1,0:T(8,128)(2,1)}) custom-call(bf16[19,128,128]{2,1,0:T(8,128)(2,1)} %shard_map.128.all_ref), custom_call_target="tpu_custom_call" | custom-call | tf_op jit(solution)/shard_map/pallas_call | solution.py:406

commit v3 on v2

--- a/solution.py
+++ b/solution.py
@@ -9,7 +9,6 @@
 
 F32 = jnp.float32
 BF = jnp.bfloat16
-COL = 9
 
 
 def tdot(a, b):
@@ -19,7 +18,7 @@
 def kernel(
     rows_ref, parent_ref, order_ref, inv_ref, p1_ref, b1_ref, p2_ref, link_ref, b2_ref,
     out_ref,
-    tf, xb, yp, fb, nb, ys, yr, gz, sc, cc, yb, dd, ar, pv1, pv2, keep, snd, rcv, loc,
+    tf, x1, x2, wb, yp, fb, nb, ys, yr, pz, lk, ub, uo, uu, ar, pv1, keep, snd, rcv, loc,
 ):
     tl = inv_ref.shape[-1]
     p = lax.axis_index("prow")
@@ -36,6 +35,7 @@
     right_z = (p, 8 * yh + 2 * zr + q)
     core = (p, 2 * j + 1 - q)
     far_y = (p, 8 * (1 - yh) + 2 * z + q)
+    far_z = (p, 8 * yh + 2 * zo + q)
 
     def held(slot):
         return 4 * (slot % 2) + (slot // 2 + z) % 4
@@ -57,32 +57,33 @@
             device_id=to, device_id_type=pl.DeviceIdType.MESH)
 
     T_AT, TURN_AT, MATE_AT, BASE_AT, FWD_AT, FWD_LEFT_AT = 0, 1, 3, 5, 13, 17
-    FAR_AT, NE_AT, NL_AT, Y_AT, G_AT, C_AT, D_AT, A_AT = 21, 29, 37, 45, 47, 51, 52, 53
+    FAR_AT, NE_AT, NL_AT, Y_AT, SWAP_AT, PZ_AT, LK_AT, UB_AT, UU_AT, A_AT = 21, 29, 37, 45, 47, 48, 52, 53, 56, 57
     panels = (p1_ref, p2_ref)
+    slots_at = (x1.at[q], x2)
 
     def turn(l):
-        return remote(panels[l].at[0], xb.at[l, to_p], TURN_AT + l, turned)
+        return remote(panels[l].at[0], slots_at[l].at[to_p], TURN_AT + l, turned)
 
     def turn_here(l):
-        return pltpu.make_async_copy(panels[l].at[0], xb.at[l, p], loc.at[l])
+        return pltpu.make_async_copy(panels[l].at[0], slots_at[l].at[p], loc.at[l])
 
     def mate(l):
-        return remote(xb.at[l, p], xb.at[l, p], MATE_AT + l, mate_y)
+        return remote(slots_at[l].at[p], slots_at[l].at[p], MATE_AT + l, mate_y)
 
     def base(t, dr):
-        at = xb.at[level[t], slot(t, x)]
+        at = slots_at[level[t]].at[slot(t, x)]
         return remote(at, at, BASE_AT + 2 * t + dr, (right_x, left_x)[dr])
 
     def base_in(t, dr):
-        at = xb.at[level[t], slot(t, (xl, xr)[dr])]
+        at = slots_at[level[t]].at[slot(t, (xl, xr)[dr])]
         return remote(at, at, BASE_AT + 2 * t + dr, right_x)
 
     def forward(t, dr):
-        at = xb.at[level[t], slot(t, (xl, xr)[dr]), pl.ds(4 * dr, 4)]
+        at = slots_at[level[t]].at[slot(t, (xl, xr)[dr]), pl.ds(4 * dr, 4)]
         return remote(at, at, FWD_AT + t, (right_x, left_x)[dr], (FWD_AT, FWD_LEFT_AT)[dr] + t)
 
     def forward_in(t):
-        at = xb.at[level[t], slot(t, xo)]
+        at = slots_at[level[t]].at[slot(t, xo)]
         return remote(at, at, FWD_AT + t, right_x)
 
     def far(t, dr):
@@ -102,9 +103,11 @@
     t_here = pltpu.make_async_copy(inv_ref, tf.at[q], loc.at[2])
     t_here.start()
     v1 = pltpu.make_async_copy(p1_ref.at[0], pv1, loc.at[3])
-    v2 = pltpu.make_async_copy(p2_ref.at[0], pv2, loc.at[4])
+    v2 = pltpu.make_async_copy(p2_ref.at[0], pz.at[z, pl.ds(0, 8)], loc.at[4])
+    v3 = pltpu.make_async_copy(link_ref.at[0], pz.at[z, 8], loc.at[5])
     v1.start()
     v2.start()
+    v3.start()
 
     barrier = pltpu.get_barrier_semaphore()
 
@@ -117,16 +120,16 @@
 
     for d in range(1, 8):
         greet(((p + d) % 8, c))
-    for to in (left_z, right_z, core, far_y):
+    for to in (left_z, right_z, core, far_y, far_z):
         greet(to)
 
     @pl.when(jnp.logical_not(stays))
     def _():
-        pl.semaphore_wait(barrier, 12)
+        pl.semaphore_wait(barrier, 13)
 
     @pl.when(stays)
     def _():
-        pl.semaphore_wait(barrier, 11)
+        pl.semaphore_wait(barrier, 12)
 
     def start_turn(l):
         @pl.when(jnp.logical_not(stays))
@@ -140,7 +143,7 @@
     def wait_turn(l):
         @pl.when(jnp.logical_not(stays))
         def _():
-            remote(xb.at[l, p], xb.at[l, p], TURN_AT + l, right_x).wait_recv()
+            remote(slots_at[l].at[p], slots_at[l].at[p], TURN_AT + l, right_x).wait_recv()
 
         @pl.when(stays)
         def _():
@@ -154,7 +157,7 @@
 
     def wait_mate(l):
         s = 2 * x + 1 - yl
-        remote(xb.at[l, s], xb.at[l, s], MATE_AT + l, right_x).wait_recv()
+        remote(slots_at[l].at[s], slots_at[l].at[s], MATE_AT + l, right_x).wait_recv()
 
     def base_out(t):
         go(base(t, 0))
@@ -175,11 +178,17 @@
         k = 2 * held(s) + q
         cols = [row_at(l, k, 8 * j + n) for n in range(8)]
         cols = [((a >> 3) & 1, a & 7) for a in cols]
+        if l == 1:
+            par = parent_ref[k]
+            at = 2 * (((par >> 1) + 4 - z) & 3) + ((par >> 3) & 1)
+            above = jnp.concatenate([x1[par & 1, at, order_ref[k, 8 * j + n] & 7] for n in range(8)], axis=0)
+            taken = jnp.dot(above, lk[s % 2, zh], preferred_element_type=F32)
+            wb[...] = (x2[s].reshape(8 * tl, tl).astype(F32) - taken).astype(BF)
 
         def one(m, carry):
             r = row_at(l, k, 8 * p + m) & 15
             wide = jnp.concatenate([tf[a, r, b] for a, b in cols], axis=1)
-            tall = xb[l, s].reshape(8 * tl, tl)
+            tall = wb[...] if l else x1[q, s].reshape(8 * tl, tl)
             yp[t, zh, m] = jnp.dot(wide, tall, preferred_element_type=F32).astype(BF)
             return carry
 
@@ -245,6 +254,20 @@
             total = total + ar[t, i].astype(F32)
         return total
 
+    def swap(s):
+        remote(x1.at[q, s], x1.at[q, s], SWAP_AT, core).start()
+
+    def swap_all():
+        return remote(x1.at[1 - q], x1.at[1 - q], SWAP_AT, core)
+
+    def child_in(dr):
+        at = pz.at[(zl, zr)[dr]]
+        return remote(at, at, PZ_AT + dr, right_z)
+
+    def child_on(dr):
+        at = pz.at[(zl, zr)[dr], pl.ds(5 * dr, 5 - dr)]
+        return remote(at, at, PZ_AT + 2, (right_z, left_z)[dr], PZ_AT + 2 + dr)
+
     start_turn(0)
     t_there = remote(inv_ref, tf.at[q], T_AT, core)
     go(t_there)
@@ -252,32 +275,54 @@
     go(mate(0))
     base_out(0)
     start_turn(1)
+    v2.wait()
+    v3.wait()
+    for dr in range(2):
+        go(remote(pz.at[z], pz.at[z], PZ_AT + dr, (right_z, left_z)[dr]))
+    swap(p)
     t_here.wait()
     t_there.wait_recv()
     products(0, x)
     wait_mate(0)
     base_out(1)
+    swap(2 * x + 1 - yl)
     relay(0)
+    swap(slot(0, xl))
+    swap(slot(0, xr))
+    for dr in range(2):
+        child_in(dr).wait_recv()
+        go(child_on(dr))
     products(1, x)
     products(0, xl)
     products(0, xr)
     wait_turn(1)
     go(mate(1))
     forward_in(0).wait_recv()
+    swap(slot(0, xo))
     products(0, xo)
     wait_mate(1)
     base_out(2)
     relay(1)
+    swap(slot(1, xl))
+    swap(slot(1, xr))
     products(1, xl)
     products(1, xr)
     pass_on(0)
     base_out(3)
+    remote(pz.at[zo], pz.at[zo], PZ_AT + 2, right_z).wait_recv()
+    for i in range(4):
+        lk[yh, i] = pz[i, 8]
+    links = remote(lk.at[yh], lk.at[yh], LK_AT, far_y)
+    go(links)
     forward_in(1).wait_recv()
+    swap(slot(1, xo))
     products(1, xo)
     relay(2)
-    products(2, x)
     meet(0)
     pass_on(1)
+    swap_all().wait_recv()
+    links.wait_recv()
+    products(2, x)
     products(3, x)
     products(2, xl)
     products(2, xr)
@@ -286,21 +331,18 @@
     forward_in(2).wait_recv()
     products(2, xo)
     v1.wait()
-    v2.wait()
 
     across(0).wait_recv()
     for m in range(8):
         tile = (-(keep[0, m] + yr[0, m].astype(F32))).astype(BF)
         out_ref[m] = tile
-        gz[z, m] = tile
-    share = tdot(pv1[...].reshape(8 * tl, tl), gz[z, pl.ds(0, 8)].reshape(8 * tl, tl))
+        ub[yh, q, m] = tile
+    share = tdot(pv1[...].reshape(8 * tl, tl), ub[yh, q, pl.ds(0, 8)].reshape(8 * tl, tl))
     ar[0, p] = share.astype(BF)
     first = jnp.where(p == 0, 1.0, 0.0).astype(F32)
-    gz[z, 8] = (b1_ref[0] * first - share).astype(BF)
-    g_right = remote(gz.at[z], gz.at[z], G_AT, right_z)
-    g_left = remote(gz.at[z], gz.at[z], G_AT + 1, left_z)
-    go(g_right)
-    go(g_left)
+    ub[yh, q, 8] = (b1_ref[0] * first - share).astype(BF)
+    go(remote(ub.at[yh, q], ub.at[yh, q], UB_AT, far_y))
+    go(remote(ub.at[yh, q], ub.at[yh, q], UB_AT + 1, core))
     spread(0)
 
     pass_on(2)
@@ -308,53 +350,49 @@
     products(3, xr)
     forward_in(3).wait_recv()
     products(3, xo)
+    remote(ub.at[1 - yh, q], ub.at[1 - yh, q], UB_AT, far_y).wait_recv()
+    go(remote(ub.at[1 - yh, q], ub.at[1 - yh, q], UB_AT + 2, core))
+    meet(2)
     pass_on(3)
-    meet(2)
-
-    remote(gz.at[zl], gz.at[zl], G_AT, right_z).wait_recv()
-    go(remote(gz.at[zl, pl.ds(0, 5)], gz.at[zl, pl.ds(0, 5)], G_AT + 2, right_z))
-    remote(gz.at[zr], gz.at[zr], G_AT + 1, right_z).wait_recv()
-    go(remote(gz.at[zr, pl.ds(5, 4)], gz.at[zr, pl.ds(5, 4)], G_AT + 2, left_z, G_AT + 3))
 
     out_ref[16] = (b1_ref[0] - spread_sum(0)).astype(BF)
 
-    remote(gz.at[zo], gz.at[zo], G_AT + 2, right_z).wait_recv()
-    for yd in range(2):
-        there = parent_ref[8 * yd + 2 * z + 1 - q]
-        sc[yd] = gz[(there >> 1) & 3]
-    to_core = remote(sc, cc.at[q], C_AT, core)
-    go(to_core)
-    for yd in range(2):
-        here = parent_ref[8 * yd + 2 * z + q]
-        cc[q, yd] = gz[(here >> 1) & 3]
-    to_core.wait_recv()
-    yb[...] = cc[parent_ref[8 * (1 - yh) + 2 * z + q] & 1, 1 - yh]
-    to_far = remote(yb, dd.at[yh], D_AT, far_y)
-    go(to_far)
-    mine = parent_ref[c]
-    dd[yh] = cc[mine & 1, yh]
+    remote(ub.at[yh, 1 - q], ub.at[yh, 1 - q], UB_AT + 1, core).wait_recv()
+    remote(ub.at[1 - yh, 1 - q], ub.at[1 - yh, 1 - q], UB_AT + 2, core).wait_recv()
+
+    def child(d, carry):
+        zc = (z + d) % 4
+        k = 8 * yh + 2 * zc + q
+        par = parent_ref[k]
+        py, pq = (par >> 3) & 1, par & 1
+        near = jnp.concatenate([ub[py, pq, order_ref[k, 8 * p + m] & 7] for m in range(8)], axis=0)
+        total = tdot(near, pz[zc, pl.ds(0, 8)].reshape(8 * tl, tl))
+        total = total + jnp.dot(ub[py, pq, 8], pz[zc, 8], preferred_element_type=F32)
+        uo[d] = total.astype(BF)
+        return carry
+
+    lax.fori_loop(0, 4, child, 0)
+    uu[z] = uo[0]
+    for d, to in ((1, right_z), (2, far_z), (3, left_z)):
+        remote(uo.at[d], uu.at[z], UU_AT, to).start()
+    uu_all = remote(uu.at[pl.ds(0, 3)], uu.at[pl.ds(0, 3)], UU_AT, far_z)
     meet(3)
-    to_far.wait_recv()
-
-    link = link_ref[0]
-    around = (mine >> 3) & 1
-    near = [dd[around, order_ref[c, 8 * p + m] & 7] for m in range(8)]
-    near_all = jnp.concatenate(near, axis=0)
-    upper = tdot(near_all, pv2[...].reshape(8 * tl, tl)) + jnp.dot(dd[around, 8], link, preferred_element_type=F32)
-    ar[1, p] = upper.astype(BF)
+    uu_all.wait_recv()
+    ar[1, p] = uu[(parent_ref[c] >> 1) & 3]
     spread(1)
-    for m in range(8):
-        keep[1, m] = keep[1, m] + jnp.dot(near[m], link, preferred_element_type=F32)
+
     across(1).wait_recv()
     for m in range(8):
         out_ref[8 + m] = (-(keep[1, m] + yr[1, m].astype(F32))).astype(BF)
-    lower = tdot(pv2[...].reshape(8 * tl, tl), out_ref[pl.ds(8, 8)].reshape(8 * tl, tl))
+    lower = tdot(pz[z, pl.ds(0, 8)].reshape(8 * tl, tl), out_ref[pl.ds(8, 8)].reshape(8 * tl, tl))
     ar[2, p] = lower.astype(BF)
     spread(2)
     u2 = (-spread_sum(1)).astype(BF)
     out_ref[17] = u2
-    rest = b2_ref[0] - tdot(link, u2)
+    rest = b2_ref[0] - tdot(pz[z, 8], u2)
     out_ref[18] = (rest - spread_sum(2)).astype(BF)
+    swap_all().wait_send()
+    uu_all.wait_send()
 
     for copy in sent:
         copy.wait_send()
@@ -391,14 +429,14 @@
     packed = pl.pallas_call(
         kernel,
         out_shape=jax.ShapeDtypeStruct((19, tl, tl), BF),
-        in_specs=[smem, smem, smem, anyw, anyw, vmem, anyw, vmem, vmem],
+        in_specs=[smem, smem, smem, anyw, anyw, vmem, anyw, anyw, vmem],
         out_specs=vmem,
         scratch_shapes=[
-            vm(2, 16, 8), vm(2, 8, 8), vm(4, 4, 8),
+            vm(2, 16, 8), vm(2, 8, 8), vm(8, 8), pltpu.VMEM((8 * tl, tl), BF), vm(4, 4, 8),
             vm(4, 2, 4), vm(4, 2, 8), vm(2, 8), vm(2, 8),
-            vm(4, COL), vm(2, COL), vm(2, 2, COL), vm(COL), vm(2, COL), vm(3, 8),
-            vm(8), vm(8), pltpu.VMEM((2, 8, tl, tl), F32),
-            pltpu.SemaphoreType.DMA((56,)), pltpu.SemaphoreType.DMA((56,)), pltpu.SemaphoreType.DMA((5,)),
+            vm(4, 9), vm(2, 4), vm(2, 2, 9), vm(4), vm(4), vm(3, 8),
+            vm(8), pltpu.VMEM((2, 8, tl, tl), F32),
+            pltpu.SemaphoreType.DMA((60,)), pltpu.SemaphoreType.DMA((60,)), pltpu.SemaphoreType.DMA((6,)),
         ],
         compiler_params=pltpu.CompilerParams(
             collective_id=0, has_side_effects=True, vmem_limit_bytes=56 * 1024 * 1024),

time: 117 us -> 103 us (0.88)
  the two profiles are of different devices: /device:TPU:53 before, /device:TPU:8 now
where the time goes in v3:
time: 103 us
  Pallas kernels  103 us (100%)
    pallas_call x1, Pallas kernels, local(): pl.pallas_call(kernel, out_shape=jax.ShapeDtypeStruct((19, tl, tl), BF),...  101 us

profile of v3, /device:TPU:8, one launch (start us, length us, event | category | flops | bytes accessed | tf_op | source)
XLA Modules:
  0.0 103.3 jit_solution(358908654679185865)
XLA Ops:
  0.6 100.7 %shard_map.128.all_ref = bf16[19,128,128]{2,1,0:T(8,128)(2,1)} custom-call(s32[16,64]{1,0:T(8,128)} %rows_ref.1, s32[16]{0:T(128)} %parent_ref.1, s32[16,64]{1,0:T(8,128)} %order_ref.1, bf16[16,8,128,128]{3,2,1,0:T(8,128)(2,1)} %inv_ref.1, bf16[1,8,128,128]{3,2,1,0:T(8,128)(2,1)} %p1_ref.1, f32[1,128,128]{2,1,0:T(8,128)} %b1_ref.1, ...), custom_call_target="tpu_custom_call" | custom-call | tf_op jit(solution)/shard_map/pallas_call | solution.py:429
  101.4 1.9 %shard_map.129 = (bf16[1,8,128,128]{3,2,1,0:T(8,128)(2,1)}, bf16[1,128,128]{2,1,0:T(8,128)(2,1)}, bf16[1,8,128,128]{3,2,1,0:T(8,128)(2,1)}, bf16[1,128,128]{2,1,0:T(8,128)(2,1)}, bf16[1,128,128]{2,1,0:T(8,128)(2,1)}) custom-call(bf16[19,128,128]{2,1,0:T(8,128)(2,1)} %shard_map.128.all_ref), custom_call_target="tpu_custom_call" | custom-call | tf_op jit(solution)/shard_map/pallas_call | solution.py:444

commit v4 on v3

--- a/solution.py
+++ b/solution.py
@@ -18,7 +18,7 @@
 def kernel(
     rows_ref, parent_ref, order_ref, inv_ref, p1_ref, b1_ref, p2_ref, link_ref, b2_ref,
     out_ref,
-    tf, x1, x2, wb, yp, fb, nb, ys, yr, pz, lk, ub, uo, uu, ar, pv1, keep, snd, rcv, loc,
+    tf, x1, x2, wb, yp, fb, nb, ys, yr, pz, lk, ub, uo, uu, ar, pr, fn, pv1, keep, snd, rcv, loc,
 ):
     tl = inv_ref.shape[-1]
     p = lax.axis_index("prow")
@@ -57,7 +57,7 @@
             device_id=to, device_id_type=pl.DeviceIdType.MESH)
 
     T_AT, TURN_AT, MATE_AT, BASE_AT, FWD_AT, FWD_LEFT_AT = 0, 1, 3, 5, 13, 17
-    FAR_AT, NE_AT, NL_AT, Y_AT, SWAP_AT, PZ_AT, LK_AT, UB_AT, UU_AT, A_AT = 21, 29, 37, 45, 47, 48, 52, 53, 56, 57
+    FAR_AT, NE_AT, NL_AT, Y_AT, SWAP_AT, PZ_AT, LK_AT, UB_AT, UU_AT, A_AT, B_AT = 21, 29, 37, 45, 47, 48, 52, 53, 56, 57, 60
     panels = (p1_ref, p2_ref)
     slots_at = (x1.at[q], x2)
 
@@ -162,6 +162,20 @@
     def base_out(t):
         go(base(t, 0))
         go(base(t, 1))
+
+    own_last = yl == yh
+
+    def both(t):
+        for dr in range(2):
+            base(t, dr).start()
+
+    def own_out():
+        pl.when(own_last)(lambda: both(3))
+        pl.when(jnp.logical_not(own_last))(lambda: both(2))
+
+    def mate_out():
+        pl.when(own_last)(lambda: both(2))
+        pl.when(jnp.logical_not(own_last))(lambda: both(3))
 
     def relay(t):
         for dr in range(2):
@@ -185,14 +199,18 @@
             taken = jnp.dot(above, lk[s % 2, zh], preferred_element_type=F32)
             wb[...] = (x2[s].reshape(8 * tl, tl).astype(F32) - taken).astype(BF)
 
-        def one(m, carry):
-            r = row_at(l, k, 8 * p + m) & 15
-            wide = jnp.concatenate([tf[a, r, b] for a, b in cols], axis=1)
+        def some(i, carry):
+            wides = []
+            for m in range(4):
+                r = row_at(l, k, 8 * p + 4 * i + m) & 15
+                wides.append(jnp.concatenate([tf[a, r, b] for a, b in cols], axis=1))
+            wide = jnp.concatenate(wides, axis=0)
             tall = wb[...] if l else x1[q, s].reshape(8 * tl, tl)
-            yp[t, zh, m] = jnp.dot(wide, tall, preferred_element_type=F32).astype(BF)
+            yp[t, zh, pl.ds(4 * i, 4)] = jnp.dot(
+                wide, tall, preferred_element_type=F32).astype(BF).reshape(4, tl, tl)
             return carry
 
-        lax.fori_loop(0, 8, one, 0)
+        lax.fori_loop(0, 8 // 4, some, 0)
 
         @pl.when(xs == 2)
         def _():
@@ -240,19 +258,37 @@
             pl.when(parity[t] != yh)(cross)
             pl.when(parity[t] == yh)(stay)
 
-    def spread(t):
+    rp = tl // 8
+
+    def rows_of(i):
+        return pl.ds(pl.multiple_of(i * rp, rp), rp)
+
+    def spread(t, value):
+        ar[t] = value
+        pr[t, p] = ar[t, rows_of(p)]
         for d in range(1, 8):
-            remote(ar.at[t, p], ar.at[t, p], A_AT + t, ((p + d) % 8, c)).start()
+            i = (p + d) % 8
+            remote(ar.at[t, rows_of(i)], pr.at[t, p], A_AT + t, (i, c)).start()
 
     def spread_all(t):
-        return remote(ar.at[t, pl.ds(0, 7)], ar.at[t, pl.ds(0, 7)], A_AT + t, right_x)
+        return remote(pr.at[t, pl.ds(0, 7)], pr.at[t, pl.ds(0, 7)], A_AT + t, right_x)
 
     def spread_sum(t):
         spread_all(t).wait_recv()
-        total = ar[t, 0].astype(F32)
+        total = pr[t, 0].astype(F32)
         for i in range(1, 8):
-            total = total + ar[t, i].astype(F32)
+            total = total + pr[t, i].astype(F32)
         return total
+
+    def hand_out(t, value):
+        fn[t, rows_of(p)] = value.astype(BF)
+        for d in range(1, 8):
+            at = fn.at[t, rows_of(p)]
+            remote(at, at, B_AT + t, ((p + d) % 8, c)).start()
+
+    def hand_all(t):
+        at = fn.at[t, pl.ds(0, 7 * rp)]
+        return remote(at, at, B_AT + t, right_x)
 
     def swap(s):
         remote(x1.at[q, s], x1.at[q, s], SWAP_AT, core).start()
@@ -269,12 +305,12 @@
         return remote(at, at, PZ_AT + 2, (right_z, left_z)[dr], PZ_AT + 2 + dr)
 
     start_turn(0)
+    start_turn(1)
     t_there = remote(inv_ref, tf.at[q], T_AT, core)
     go(t_there)
     wait_turn(0)
     go(mate(0))
     base_out(0)
-    start_turn(1)
     v2.wait()
     v3.wait()
     for dr in range(2):
@@ -297,18 +333,18 @@
     products(0, xr)
     wait_turn(1)
     go(mate(1))
+    own_out()
     forward_in(0).wait_recv()
     swap(slot(0, xo))
     products(0, xo)
+    relay(1)
     wait_mate(1)
-    base_out(2)
-    relay(1)
+    mate_out()
     swap(slot(1, xl))
     swap(slot(1, xr))
     products(1, xl)
     products(1, xr)
     pass_on(0)
-    base_out(3)
     remote(pz.at[zo], pz.at[zo], PZ_AT + 2, right_z).wait_recv()
     for i in range(4):
         lk[yh, i] = pz[i, 8]
@@ -338,12 +374,11 @@
         out_ref[m] = tile
         ub[yh, q, m] = tile
     share = tdot(pv1[...].reshape(8 * tl, tl), ub[yh, q, pl.ds(0, 8)].reshape(8 * tl, tl))
-    ar[0, p] = share.astype(BF)
     first = jnp.where(p == 0, 1.0, 0.0).astype(F32)
     ub[yh, q, 8] = (b1_ref[0] * first - share).astype(BF)
     go(remote(ub.at[yh, q], ub.at[yh, q], UB_AT, far_y))
     go(remote(ub.at[yh, q], ub.at[yh, q], UB_AT + 1, core))
-    spread(0)
+    spread(0, share.astype(BF))
 
     pass_on(2)
     products(3, xl)
@@ -355,7 +390,7 @@
     meet(2)
     pass_on(3)
 
-    out_ref[16] = (b1_ref[0] - spread_sum(0)).astype(BF)
+    hand_out(0, b1_ref[0, rows_of(p)] - spread_sum(0))
 
     remote(ub.at[yh, 1 - q], ub.at[yh, 1 - q], UB_AT + 1, core).wait_recv()
     remote(ub.at[1 - yh, 1 - q], ub.at[1 - yh, 1 - q], UB_AT + 2, core).wait_recv()
@@ -378,22 +413,26 @@
     uu_all = remote(uu.at[pl.ds(0, 3)], uu.at[pl.ds(0, 3)], UU_AT, far_z)
     meet(3)
     uu_all.wait_recv()
-    ar[1, p] = uu[(parent_ref[c] >> 1) & 3]
-    spread(1)
+    upper = uu[(parent_ref[c] >> 1) & 3]
+    spread(1, upper)
+    linked = tdot(pz[z, 8], upper)
 
     across(1).wait_recv()
     for m in range(8):
         out_ref[8 + m] = (-(keep[1, m] + yr[1, m].astype(F32))).astype(BF)
     lower = tdot(pz[z, pl.ds(0, 8)].reshape(8 * tl, tl), out_ref[pl.ds(8, 8)].reshape(8 * tl, tl))
-    ar[2, p] = lower.astype(BF)
-    spread(2)
-    u2 = (-spread_sum(1)).astype(BF)
-    out_ref[17] = u2
-    rest = b2_ref[0] - tdot(pz[z, 8], u2)
-    out_ref[18] = (rest - spread_sum(2)).astype(BF)
+    spread(2, (lower - linked).astype(BF))
+    hand_out(1, -spread_sum(1))
+    hand_out(2, b2_ref[0, rows_of(p)] - spread_sum(2))
+    for t in range(3):
+        hand_all(t).wait_recv()
+        out_ref[16 + t] = fn[t]
     swap_all().wait_send()
     uu_all.wait_send()
 
+    for t in (2, 3):
+        for dr in range(2):
+            base(t, dr).wait_send()
     for copy in sent:
         copy.wait_send()
     for l in range(2):
@@ -408,6 +447,7 @@
             near_early(t, dr).wait_send()
     for t in range(3):
         spread_all(t).wait_send()
+        hand_all(t).wait_send()
 
 
 def unpack(all_ref, c1_ref, d1_ref, c2_ref, u2_ref, d2_ref):
@@ -434,9 +474,9 @@
         scratch_shapes=[
             vm(2, 16, 8), vm(2, 8, 8), vm(8, 8), pltpu.VMEM((8 * tl, tl), BF), vm(4, 4, 8),
             vm(4, 2, 4), vm(4, 2, 8), vm(2, 8), vm(2, 8),
-            vm(4, 9), vm(2, 4), vm(2, 2, 9), vm(4), vm(4), vm(3, 8),
+            vm(4, 9), vm(2, 4), vm(2, 2, 9), vm(4), vm(4), vm(3), pltpu.VMEM((3, 8, tl // 8, tl), BF), vm(3),
             vm(8), pltpu.VMEM((2, 8, tl, tl), F32),
-            pltpu.SemaphoreType.DMA((60,)), pltpu.SemaphoreType.DMA((60,)), pltpu.SemaphoreType.DMA((6,)),
+            pltpu.SemaphoreType.DMA((63,)), pltpu.SemaphoreType.DMA((63,)), pltpu.SemaphoreType.DMA((6,)),
         ],
         compiler_params=pltpu.CompilerParams(
             collective_id=0, has_side_effects=True, vmem_limit_bytes=56 * 1024 * 1024),

time: 103 us -> 94.6 us (0.918)
  Pallas kernels: 103 us -> 93.5 us
    pallas_call x1, Pallas kernels: 101 us -> 91.6 us  [local(): pl.pallas_call(kernel, out_shape=jax.ShapeDtypeStruct((19, tl, tl), BF),...]
where the time goes in v4:
time: 94.6 us; the launch traced here: 94.1 us
  Pallas kernels  93.5 us (99%)
    pallas_call x1, Pallas kernels, local(): pl.pallas_call(kernel, out_shape=jax.ShapeDtypeStruct((19, tl, tl), BF),...  91.6 us
    pallas_call x1, Pallas kernels, local(): pl.pallas_call(unpack, out_shape=(one, tile, one, tile, tile), in_specs=[...  1.89 us

profile of v4, /device:TPU:8, one launch (start us, length us, event | category | flops | bytes accessed | tf_op | source)
XLA Modules:
  0.0 94.1 jit_solution(3570813613472927533)
XLA Ops:
  0.6 91.6 %shard_map.128.all_ref = bf16[19,128,128]{2,1,0:T(8,128)(2,1)} custom-call(s32[16,64]{1,0:T(8,128)} %rows_ref.1, s32[16]{0:T(128)} %parent_ref.1, s32[16,64]{1,0:T(8,128)} %order_ref.1, bf16[16,8,128,128]{3,2,1,0:T(8,128)(2,1)} %inv_ref.1, bf16[1,8,128,128]{3,2,1,0:T(8,128)(2,1)} %p1_ref.1, f32[1,128,128]{2,1,0:T(8,128)} %b1_ref.1, ...), custom_call_target="tpu_custom_call" | custom-call | tf_op jit(solution)/shard_map/pallas_call | solution.py:469
  92.2 1.9 %shard_map.129 = (bf16[1,8,128,128]{3,2,1,0:T(8,128)(2,1)}, bf16[1,128,128]{2,1,0:T(8,128)(2,1)}, bf16[1,8,128,128]{3,2,1,0:T(8,128)(2,1)}, bf16[1,128,128]{2,1,0:T(8,128)(2,1)}, bf16[1,128,128]{2,1,0:T(8,128)(2,1)}) custom-call(bf16[19,128,128]{2,1,0:T(8,128)(2,1)} %shard_map.128.all_ref), custom_call_target="tpu_custom_call" | custom-call | tf_op jit(solution)/shard_map/pallas_call | solution.py:484
